TPU v7x, 32 devices: a whole 2x2x4 slice. The times are simulated.
32 devices in a mesh: groups: 2 (over y), rows: 4 (over z), mp: 2 (over x), pair: 2 (over core).
Axes of the slice: x: 2, y: 2, z: 4, core: 2. Of those that a mesh axis runs over, the one named last changes fastest.
Arguments:
- query_rows: bfloat16 [2048, 512], P(('groups', 'rows', 'pair'), 'mp'), parts along dimension 0, may hold values from -240 to 240
- key_rows: bfloat16 [65536, 512], P(('groups', 'rows', 'pair'), 'mp'), parts along dimension 0, may hold values from -24 to 24
- value_rows: bfloat16 [65536, 512], P(('groups', 'rows', 'pair'), 'mp'), parts along dimension 0, may hold values from -6 to 6
- cotangent: bfloat16 [2048, 512], P(('groups', 'rows', 'pair'), 'mp'), parts along dimension 0, may hold values from -1536 to 1536
- train_rows: int32 [16], P('groups'), parts along dimension 0, may hold values from 1 to 12288, as said below
- test_rows: int32 [16], P('groups'), parts along dimension 0, may hold values from 32 to 128
- block_table: int32 [128], P('groups'), parts along dimension 0, may hold values from 0 to 7, as said below
Outputs:
- query_grad: bfloat16 [2048, 512], P(('groups', 'rows', 'pair'), 'mp'), parts along dimension 0
- key_grad: bfloat16 [65536, 512], P(('groups', 'rows', 'pair'), 'mp'), parts along dimension 0
- value_grad: bfloat16 [65536, 512], P(('groups', 'rows', 'pair'), 'mp'), parts along dimension 0
There are 2 independent parts, one for each index of `groups`. A program takes and returns all parts, laid end to end along the dimension named above; each array names one. Nothing has to cross between parts.
Inputs may be any that keep to these rules, and one draw needn't show every extreme that they name: block_table names table t exactly ceil(train_rows[t] / 512) times; the largest table has 24 full blocks. `block_table`: every table is named at least once.
All inputs are finite; a program needn't handle non-finite values.
Results may differ from a plain program's by a relative error of at most 0.0075.
Values may be sent and summed in bfloat16 or wider, within the bound.
No kernel may reach another device: no remote copies, remote signals or barrier semaphores. Data moves between devices by JAX's collectives and lax.ppermute only.
A program may use at most 64 MiB of HBM per device.

v0:
```python
import math
import jax
import jax.numpy as jnp
from jax import lax
from jax.sharding import PartitionSpec as P

HD = 64
TEST = 128
BLK = 512
NEG = -1e30


def combined_all(value, axis, join):
    pieces = jax.tree.map(lambda part: lax.all_gather(part, axis), value)
    head = jax.tree.map(lambda part: part[0], pieces)
    tail = jax.tree.map(lambda part: part[1:], pieces)
    total, _ = lax.scan(lambda total, piece: (join(total, piece), None), head, tail)
    return total


def table_lookup(positions, entries):
    matches = positions[:, None] == jnp.arange(entries.shape[0], dtype=jnp.int32)[None, :]
    return jnp.sum(jnp.where(matches, entries[None, :], 0), axis=1)


def merge_two(former, latter):
    new_peak = jnp.maximum(former[0], latter[0])
    return (
        new_peak,
        former[1] * jnp.exp(former[0] - new_peak) + latter[1] * jnp.exp(latter[0] - new_peak),
    )


def contract_rows(left, right):
    return lax.dot_general(
        left, right, (((0,), (0,)), ((), ())), preferred_element_type=jnp.float32
    )


def contract_features(left, right):
    return lax.dot_general(
        left, right, (((1,), (1,)), ((), ())), preferred_element_type=jnp.float32
    )


def local(query_rows, key_rows, value_rows, cotangent, train_rows, test_rows, block_table):
    device = lax.axis_index(("rows", "pair"))
    local_rows = query_rows.shape[0]
    features = query_rows.shape[1]
    head_count = features // HD
    blocks = key_rows.shape[0] // BLK
    tables = train_rows.shape[0]
    query_count = tables * TEST
    stacked = head_count * TEST
    score_scale = 1.0 / math.sqrt(HD)
    row_ids = device * local_rows + jnp.arange(local_rows, dtype=jnp.int32)
    query_live = row_ids % TEST < table_lookup(row_ids // TEST, test_rows)
    live_grads = jnp.where(query_live[:, None], cotangent, jnp.zeros_like(cotangent))
    all_queries, all_grads = (
        lax.all_gather(query_rows, ("rows", "pair"), axis=0, tiled=True),
        lax.all_gather(live_grads, ("rows", "pair"), axis=0, tiled=True),
    )
    head_of_feature = jnp.arange(features, dtype=jnp.int32) // HD
    head_mask = head_of_feature[None, :] == jnp.arange(head_count, dtype=jnp.int32)[:, None]

    def expand(rows):
        shaped = rows.reshape(tables, 1, TEST, features)
        masked = jnp.where(head_mask[None, :, None, :], shaped, jnp.zeros_like(shaped))
        return masked.reshape(tables, stacked, features)

    def collapse(product):
        shaped = product.reshape(head_count, TEST, features)
        return jnp.sum(jnp.where(head_mask[:, None, :], shaped, 0.0), axis=0)

    spread_queries = expand(all_queries)
    spread_grads = expand(all_grads)
    block_ids = jnp.arange(block_table.shape[0], dtype=jnp.int32)
    my_blocks = device * blocks + jnp.arange(blocks, dtype=jnp.int32)
    block_owner = lax.dynamic_slice_in_dim(block_table, device * blocks, blocks)
    earlier = (block_table[None, :] == block_owner[:, None]) & (
        block_ids[None, :] < my_blocks[:, None]
    )
    ordinal = jnp.sum(jnp.where(earlier, 1, 0), axis=1).astype(jnp.int32)
    live_keys = table_lookup(block_owner, train_rows) - ordinal * BLK
    key_blocks = key_rows.reshape(blocks, BLK, features)
    value_blocks = value_rows.reshape(blocks, BLK, features)
    key_index = jnp.arange(BLK, dtype=jnp.int32)
    block_inputs = (block_owner, live_keys, key_blocks, value_blocks)

    def block_scores(which_table, live_count, key_block):
        query_block = spread_queries[which_table]
        raw_scores = contract_features(query_block, key_block) * score_scale
        return (query_block, jnp.where(key_index[None, :] < live_count, raw_scores, NEG))

    def stats_step(running, inputs):
        which_table, live_count, key_block, value_block = inputs
        _, scores = block_scores(which_table, live_count, key_block)
        block_peak = jnp.max(scores, axis=1)
        weights = jnp.exp(scores - block_peak[:, None])
        block_mass = jnp.sum(weights, axis=1)
        old_peak = running[0][which_table]
        old_mass = running[1][which_table]
        new_peak = jnp.maximum(old_peak, block_peak)
        old_weight = jnp.exp(old_peak - new_peak)
        new_weight = jnp.exp(block_peak - new_peak)
        updated = [
            running[0].at[which_table].set(new_peak),
            running[1].at[which_table].set(old_mass * old_weight + block_mass * new_weight),
        ]
        return (tuple(updated), None)

    initial = [
        jnp.full((tables, stacked), NEG, jnp.float32),
        jnp.zeros((tables, stacked), jnp.float32),
    ]
    result, _ = lax.scan(stats_step, tuple(initial), block_inputs)
    peaks, masses = result
    peaks, masses = combined_all((peaks, masses), ("rows", "pair"), merge_two)

    def inner_step(running, inputs):
        which_table, live_count, key_block, value_block = inputs
        _, scores = block_scores(which_table, live_count, key_block)
        dprobs = contract_features(spread_grads[which_table], value_block)
        block_peak = jnp.max(scores, axis=1)
        weights_low = jnp.exp(scores - block_peak[:, None]).astype(jnp.bfloat16).astype(jnp.float32)
        term = (
            jnp.sum(weights_low * dprobs, axis=1)
            * jnp.exp(block_peak - peaks[which_table])
            / masses[which_table]
        )
        return (running.at[which_table].add(term), None)

    inner_terms, _ = lax.scan(inner_step, jnp.zeros((tables, stacked), jnp.float32), block_inputs)
    inner = lax.psum(inner_terms, ("rows", "pair"))

    def grad_step(running, inputs):
        which_table, live_count, key_block, value_block = inputs
        query_block, scores = block_scores(which_table, live_count, key_block)
        grad_block = spread_grads[which_table]
        probs = jnp.exp(scores - peaks[which_table][:, None]) / masses[which_table][:, None]
        dprobs = contract_features(grad_block, value_block)
        probs_low = probs.astype(jnp.bfloat16)
        value_part = contract_rows(probs_low, grad_block)
        dscores = (probs * (dprobs - inner[which_table][:, None])).astype(jnp.bfloat16)
        key_part = contract_rows(dscores, query_block) * score_scale
        query_part = (
            collapse(jnp.dot(dscores, key_block, preferred_element_type=jnp.float32)) * score_scale
        )
        running = running.at[which_table].add(query_part)
        return (running, (key_part.astype(jnp.bfloat16), value_part.astype(jnp.bfloat16)))

    query_terms, (key_parts, value_parts) = lax.scan(
        grad_step, jnp.zeros((tables, TEST, features), jnp.float32), block_inputs
    )
    query_total = lax.psum_scatter(
        query_terms.reshape(query_count, features),
        ("rows", "pair"),
        scatter_dimension=0,
        tiled=True,
    )
    return (
        query_total.astype(jnp.bfloat16),
        key_parts.reshape(blocks * BLK, features),
        value_parts.reshape(blocks * BLK, features),
    )


def solution(mesh):
    in_specs = (
        P(("groups", "rows", "pair"), "mp"),
        P(("groups", "rows", "pair"), "mp"),
        P(("groups", "rows", "pair"), "mp"),
        P(("groups", "rows", "pair"), "mp"),
        P("groups"),
        P("groups"),
        P("groups"),
    )
    out_specs = (
        P(("groups", "rows", "pair"), "mp"),
        P(("groups", "rows", "pair"), "mp"),
        P(("groups", "rows", "pair"), "mp"),
    )
    return jax.shard_map(local, mesh=mesh, in_specs=in_specs, out_specs=out_specs, check_vma=False)
```

profile of v0, /device:TPU:0, one launch (start us, length us, event | category | flops | bytes accessed | tf_op | source)
XLA Modules:
  0.0 357.1 jit_solution(11898617688526695184)
XLA Ops:
  11.4 16.6 %all_gather.23 = bf16[1024,256]{1,0:T(8,128)(2,1)S(1)} all-gather(bf16[128,256]{1,0:T(8,128)(2,1)S(1)} %broadcast_select_fusion.3), channel_id=1, replica_groups=mesh['groups'=2,'rows'=4,'mp'=2,'pair'=2] {'rows','pair'}, dimensions={0}, use_global_device_ids=true | all-gather | bytes 589824 | tf_op jit(solution)/shard_map/all_gather | solution.py:61
  28.0 14.9 %all_gather.18 = bf16[1024,256]{1,0:T(8,128)(2,1)S(1)} all-gather(bf16[128,256]{1,0:T(8,128)(2,1)} %param.23), channel_id=1, replica_groups=mesh['groups'=2,'rows'=4,'mp'=2,'pair'=2] {'rows','pair'}, dimensions={0}, use_global_device_ids=true | all-gather | bytes 589824 | tf_op jit(solution)/shard_map/all_gather | solution.py:60
  42.9 1.7 bitcast_select_fusion
  44.6 55.1 %while.60 = (s32[]{:T(128)}, f32[8,512]{1,0:T(8,128)S(1)}, f32[8,512]{1,0:T(8,128)S(1)}, s32[8]{0:T(128)S(1)}, s32[8]{0:T(128)S(1)}, /*index=5*/bf16[8,512,256]{...) while((s32[]{:T(128)}, f32[8,512]{1,0:T(8,128)S(1)}, ...), condition=%wide.region_7.8_spmd.clone.clone, body=%wide.region_3.7_spmd.clone.sunk.clone | while | flops 135532048 | bytes 2649797 | solution.py:116
  49.2 1.4 fusion.112
  56.0 1.4 fusion.112
  62.9 1.4 fusion.112
  69.8 1.4 fusion.112
  76.7 1.4 fusion.112
  83.6 1.4 fusion.112
  90.5 1.4 fusion.112
  97.4 1.4 fusion.112
  99.8 14.2 %all-gather.1 = f32[64,512]{1,0:T(8,128)S(1)} all-gather(f32[8,512]{1,0:T(8,128)S(1)} %get-tuple-element.259), channel_id=3, replica_groups=mesh['groups'=2,'rows'=4,'mp'=2,'pair'=2] {'rows','pair'}, dimensions={0}, use_global_device_ids=true | all-gather | bytes 147456 | tf_op jit(solution)/shard_map/all_gather | solution.py:14
  114.0 14.0 %all-gather = f32[64,512]{1,0:T(8,128)S(1)} all-gather(f32[8,512]{1,0:T(8,128)S(1)} %get-tuple-element.258), channel_id=2, replica_groups=mesh['groups'=2,'rows'=4,'mp'=2,'pair'=2] {'rows','pair'}, dimensions={0}, use_global_device_ids=true | all-gather | bytes 147456 | tf_op jit(solution)/shard_map/all_gather | solution.py:14
  128.3 61.7 %while.61 = (s32[]{:T(128)}, f32[8,512]{1,0:T(8,128)S(1)}, s32[8]{0:T(128)S(1)}, s32[8]{0:T(128)S(1)}, bf16[8,512,256]{2,1,0:T(8,128)(2,1)}, /*index=5*/bf16[8,5...) while((s32[]{:T(128)}, f32[8,512]{1,0:T(8,128)S(1)}, ...), condition=%wide.region_14.15_spmd.clone.clone, body=%wide.region_10.14_spmd.clone.sunk.clone | while | flops 270534656 | bytes 3170525 | solution.py:133
  132.6 1.4 fusion.115
  134.0 1.3 fusion.116
  140.3 1.4 fusion.115
  141.7 1.3 fusion.116
  148.1 1.4 fusion.115
  149.4 1.3 fusion.116
  155.8 1.4 fusion.115
  163.5 1.4 fusion.115
  164.9 1.3 fusion.116
  171.2 1.4 fusion.115
  172.6 1.3 fusion.116
  178.9 1.4 fusion.115
  186.6 1.4 fusion.115
  190.1 29.2 %psum.7 = f32[8,512]{1,0:T(8,128)S(1)} all-reduce(f32[8,512]{1,0:T(8,128)S(1)} %get-tuple-element.262), channel_id=1, replica_groups=mesh['groups'=2,'rows'=4,'mp'=2,'pair'=2] {'rows','pair'}, use_global_device_ids=true, to_apply=%region_15.16 | all-reduce | flops 4096 | bytes 32768 | tf_op jit(solution)/shard_map/psum | solution.py:134
  219.4 97.7 %while.62 = (s32[]{:T(128)}, f32[8,128,256]{2,1,0:T(8,128)S(1)}, bf16[8,512,256]{2,1,0:T(8,128)(2,1)}, bf16[8,512,256]{2,1,0:T(8,128)(2,1)}, s32[8]{0:T(128)S(1)...) while((s32[]{:T(128)}, f32[8,128,256]{2,1,0:T(8,128)S(1)}, ...), condition=%wide.region_19.20_spmd.clone.clone, body=%wide.region_16.19_spmd.clone.sunk.clone | while | flops 673908224 | bytes 7627025 | solution.py:152
  223.8 1.5 fusion.127
  229.6 2.0 fusion.131
  236.0 1.5 fusion.127
  241.8 2.0 fusion.131
  248.3 1.5 fusion.127
  254.0 2.0 fusion.131
  260.5 1.5 fusion.127
  266.2 2.0 fusion.131
  272.7 1.5 fusion.127
  278.4 2.0 fusion.131
  284.9 1.5 fusion.127
  290.6 2.0 fusion.131
  297.1 1.5 fusion.127
  302.9 2.0 fusion.131
  309.3 1.5 fusion.127
  315.1 2.0 fusion.131
  318.1 30.6 %reduce-scatter.2.cloned.1.call-done = f32[128,256]{1,0:T(8,128)} async-done(((f32[1024,256]{1,0:T(8,128)}), f32[128,256]{1,0:T(8,128)}) %reduce-scatter.2.cloned.1.call-update) | async-done | bytes 131088 | tf_op jit(solution)/shard_map/reduce_scatter | solution.py:155
  348.7 1.5 convert_element_type.21
  (241 shorter events, 118.2 us)
Async XLA Ops:
  7.2 341.5 %reduce-scatter.2.cloned.1.call-start = ((), (), s32[]{:S(2)}) async-start(), calls=%async_computation.1 | async-start | bytes 1179648 | tf_op jit(solution)/shard_map/reduce_scatter | solution.py:155
  42.9 1.7 copy-start.1
  128.3 91.1 %copy-start.2 = (s32[3]{0:T(128)S(1)}, s32[3]{0:T(128)}, u32[]{:S(2)}) copy-start(s32[3]{0:T(128)} %constant.200.clone.2) | copy-start | bytes 40
  317.1 1.0 copy-start
Sparse Core Ops, SparseCore 0:
  318.2 30.4 reduce-scatter.1
where the time goes:
time: 360 us; the launch traced here: 357 us
  matrix products  89.4 us (25%)
  blocking collectives  89 us (25%)
  other arithmetic  55.6 us (15%)
  loops' own time  45.8 us (13%)
  local copies, waits for them, and re-layouts  32.5 us (9%)
  waiting for transfers between devices  30.6 us (8%)
  between operations  14.2 us (4%)
    dot_general x40, matrix products, contract_features(): lax.dot_general(left, right, (((1,), (1,)), ((), ())), preferred_element_...  54.7 us
    reduce_scatter x1, waiting for transfers between devices, local(): lax.psum_scatter(query_terms.reshape(query_count, features), ('rows', 'pa...  30.6 us
    psum x1, blocking collectives, local(): inner = lax.psum(inner_terms, ('rows', 'pair'))  29.2 us
    dynamic_slice x48, local copies, waits for them, and re-layouts, local(): result, _ = lax.scan(stats_step, tuple(initial), block_inputs)  29 us
    all_gather x2, blocking collectives, combined_all(): pieces = jax.tree.map(lambda part: lax.all_gather(part, axis), value)  28.2 us
    another operation x42, other arithmetic  27.8 us
    dot_general x16, matrix products, contract_rows(): lax.dot_general(left, right, (((0,), (0,)), ((), ())), preferred_element_...  24.6 us
    all_gather x1, blocking collectives, local(): lax.all_gather(live_grads, ('rows', 'pair'), axis=0, tiled=True)  16.6 us
  transfers between devices with their start and end apart: 1, of which 1 were waited for; matrix products, arithmetic and copies ran while one was open for 0% of the time, Pallas kernels for 0%

commit v1 on v0

--- a/solution.py
+++ b/solution.py
@@ -44,6 +44,25 @@
 
 
 def local(query_rows, key_rows, value_rows, cotangent, train_rows, test_rows, block_table):
+
+    def cover_links(page):
+        a_name = ("rows", "pair")
+        spare = lax.axis_size(a_name)
+        h_now = lax.axis_index(a_name)
+        all_rows, inter, kept_arr = (spare, h_now, page.shape[0])
+        stack_in = [d * all_rows if k == 0 else d for k, d in enumerate(page.shape)]
+        item_now = jnp.zeros(stack_in, page.dtype)
+        local_next = lax.dynamic_update_slice_in_dim(item_now, page, inter * kept_arr, axis=0)
+        for pp in range(1, all_rows):
+            block_now = range(all_rows)
+            heard = map(lambda k: (k, (k + 1) % all_rows), block_now)
+            met_up = list(heard)
+            page = lax.ppermute(page, a_name, met_up)
+            local_next = lax.dynamic_update_slice_in_dim(
+                local_next, page, (inter - pp) % all_rows * kept_arr, axis=0
+            )
+        return local_next
+
     device = lax.axis_index(("rows", "pair"))
     local_rows = query_rows.shape[0]
     features = query_rows.shape[1]
@@ -57,7 +76,7 @@
     query_live = row_ids % TEST < table_lookup(row_ids // TEST, test_rows)
     live_grads = jnp.where(query_live[:, None], cotangent, jnp.zeros_like(cotangent))
     all_queries, all_grads = (
-        lax.all_gather(query_rows, ("rows", "pair"), axis=0, tiled=True),
+        cover_links(query_rows),
         lax.all_gather(live_grads, ("rows", "pair"), axis=0, tiled=True),
     )
     head_of_feature = jnp.arange(features, dtype=jnp.int32) // HD

time: 360 us -> 376 us (1.044)
  waiting for transfers between devices: 30.6 us -> 63.1 us
  blocking collectives: 89 us -> 70.8 us
    ppermute x0 -> x7, waiting for transfers between devices: none -> 32.5 us  [cover_links(): page = lax.ppermute(page, a_name, met_up)]
    all_gather x1 -> x0, blocking collectives: 14.9 us -> none  [local(): lax.all_gather(query_rows, ('rows', 'pair'), axis=0, tiled=True)]
  transfers between devices with their start and end apart: 1 -> 8, of which waited for: 1 -> 7; matrix products, arithmetic and copies ran while one was open for 0% -> 1% of each run, Pallas kernels for 0% -> 0%
where the time goes in v1:
time: 376 us; the launch traced here: 373 us
  matrix products  89.4 us (24%)
  blocking collectives  70.8 us (19%)
  waiting for transfers between devices  63.1 us (17%)
  other arithmetic  55.6 us (15%)
  loops' own time  45.8 us (12%)
  local copies, waits for them, and re-layouts  33.5 us (9%)
  between operations  14.2 us (4%)
    dot_general x40, matrix products, contract_features(): lax.dot_general(left, right, (((1,), (1,)), ((), ())), preferred_element_...  54.7 us
    ppermute x7, waiting for transfers between devices, cover_links(): page = lax.ppermute(page, a_name, met_up)  32.5 us
    reduce_scatter x1, waiting for transfers between devices, local(): lax.psum_scatter(query_terms.reshape(query_count, features), ('rows', 'pa...  30.6 us
    dynamic_slice x48, local copies, waits for them, and re-layouts, local(): result, _ = lax.scan(stats_step, tuple(initial), block_inputs)  29 us
    all_gather x2, blocking collectives, combined_all(): pieces = jax.tree.map(lambda part: lax.all_gather(part, axis), value)  27.9 us
    another operation x42, other arithmetic  27.8 us
    psum x1, blocking collectives, local(): inner = lax.psum(inner_terms, ('rows', 'pair'))  26.1 us
    dot_general x16, matrix products, contract_rows(): lax.dot_general(left, right, (((0,), (0,)), ((), ())), preferred_element_...  24.6 us
  transfers between devices with their start and end apart: 8, of which 7 were waited for; matrix products, arithmetic and copies ran while one was open for 1% of the time, Pallas kernels for 0%

profile of v1, /device:TPU:0, one launch (start us, length us, event | category | flops | bytes accessed | tf_op | source)
XLA Modules:
  0.0 373.3 jit_solution(6385626040197426120)
XLA Ops:
  11.9 16.7 %all_gather.19 = bf16[1024,256]{1,0:T(8,128)(2,1)S(1)} all-gather(bf16[128,256]{1,0:T(8,128)(2,1)S(1)} %broadcast_select_fusion.3), channel_id=1, replica_groups=mesh['groups'=2,'rows'=4,'mp'=2,'pair'=2] {'rows','pair'}, dimensions={0}, use_global_device_ids=true | all-gather | bytes 589824 | tf_op jit(solution)/shard_map/all_gather | solution.py:80
  29.9 5.1 %collective-permute-done.1 = bf16[128,256]{1,0:T(8,128)(2,1)S(1)} collective-permute-done((bf16[128,256]{1,0:T(8,128)(2,1)S(1)}, bf16[128,256]{1,0:T(8,128)(2,1)S(1)}, u32[]{:S(2)}, u32[]{:S(2)}) %collective-permute-start.1) | collective-permute-done | bytes 65568 | tf_op jit(solution)/shard_map/ppermute | solution.py:60
  35.0 5.5 %collective-permute-done.2 = bf16[128,256]{1,0:T(8,128)(2,1)S(1)} collective-permute-done((bf16[128,256]{1,0:T(8,128)(2,1)S(1)}, bf16[128,256]{1,0:T(8,128)(2,1)S(1)}, u32[]{:S(2)}, u32[]{:S(2)}) %collective-permute-start.2) | collective-permute-done | bytes 65568 | tf_op jit(solution)/shard_map/ppermute | solution.py:60
  40.5 5.5 %collective-permute-done.3 = bf16[128,256]{1,0:T(8,128)(2,1)S(1)} collective-permute-done((bf16[128,256]{1,0:T(8,128)(2,1)S(1)}, bf16[128,256]{1,0:T(8,128)(2,1)S(1)}, u32[]{:S(2)}, u32[]{:S(2)}) %collective-permute-start.3) | collective-permute-done | bytes 65568 | tf_op jit(solution)/shard_map/ppermute | solution.py:60
  46.0 5.5 %collective-permute-done.4 = bf16[128,256]{1,0:T(8,128)(2,1)S(1)} collective-permute-done((bf16[128,256]{1,0:T(8,128)(2,1)S(1)}, bf16[128,256]{1,0:T(8,128)(2,1)S(1)}, u32[]{:S(2)}, u32[]{:S(2)}) %collective-permute-start.4) | collective-permute-done | bytes 65568 | tf_op jit(solution)/shard_map/ppermute | solution.py:60
  51.5 5.5 %collective-permute-done.5 = bf16[128,256]{1,0:T(8,128)(2,1)S(1)} collective-permute-done((bf16[128,256]{1,0:T(8,128)(2,1)S(1)}, bf16[128,256]{1,0:T(8,128)(2,1)S(1)}, u32[]{:S(2)}, u32[]{:S(2)}) %collective-permute-start.5) | collective-permute-done | bytes 65568 | tf_op jit(solution)/shard_map/ppermute | solution.py:60
  57.0 5.5 %collective-permute-done.6 = bf16[128,256]{1,0:T(8,128)(2,1)S(1)} collective-permute-done((bf16[128,256]{1,0:T(8,128)(2,1)S(1)}, bf16[128,256]{1,0:T(8,128)(2,1)S(1)}, u32[]{:S(2)}, u32[]{:S(2)}) %collective-permute-start.6) | collective-permute-done | bytes 65568 | tf_op jit(solution)/shard_map/ppermute | solution.py:60
  62.6 1.7 bitcast_select_fusion
  64.3 55.1 %while.60 = (s32[]{:T(128)}, f32[8,512]{1,0:T(8,128)S(1)}, f32[8,512]{1,0:T(8,128)S(1)}, s32[8]{0:T(128)S(1)}, s32[8]{0:T(128)S(1)}, /*index=5*/bf16[8,512,256]{...) while((s32[]{:T(128)}, f32[8,512]{1,0:T(8,128)S(1)}, ...), condition=%wide.region_7.8_spmd.clone.clone, body=%wide.region_3.7_spmd.clone.sunk.clone | while | flops 135532048 | bytes 2649797 | solution.py:135
  68.8 1.4 fusion.112
  75.6 1.4 fusion.112
  82.5 1.4 fusion.112
  89.4 1.4 fusion.112
  96.3 1.4 fusion.112
  103.2 1.4 fusion.112
  110.1 1.4 fusion.112
  117.0 1.4 fusion.112
  119.4 14.0 %all-gather.1 = f32[64,512]{1,0:T(8,128)S(1)} all-gather(f32[8,512]{1,0:T(8,128)S(1)} %get-tuple-element.259), channel_id=3, replica_groups=mesh['groups'=2,'rows'=4,'mp'=2,'pair'=2] {'rows','pair'}, dimensions={0}, use_global_device_ids=true | all-gather | bytes 147456 | tf_op jit(solution)/shard_map/all_gather | solution.py:14
  133.3 14.0 %all-gather = f32[64,512]{1,0:T(8,128)S(1)} all-gather(f32[8,512]{1,0:T(8,128)S(1)} %get-tuple-element.258), channel_id=2, replica_groups=mesh['groups'=2,'rows'=4,'mp'=2,'pair'=2] {'rows','pair'}, dimensions={0}, use_global_device_ids=true | all-gather | bytes 147456 | tf_op jit(solution)/shard_map/all_gather | solution.py:14
  147.7 61.7 %while.61 = (s32[]{:T(128)}, f32[8,512]{1,0:T(8,128)S(1)}, s32[8]{0:T(128)S(1)}, s32[8]{0:T(128)S(1)}, bf16[8,512,256]{2,1,0:T(8,128)(2,1)}, /*index=5*/bf16[8,5...) while((s32[]{:T(128)}, f32[8,512]{1,0:T(8,128)S(1)}, ...), condition=%wide.region_14.15_spmd.clone.clone, body=%wide.region_10.14_spmd.clone.sunk.clone | while | flops 270534656 | bytes 3170525 | solution.py:152
  152.0 1.4 fusion.115
  159.7 1.4 fusion.115
  167.4 1.4 fusion.115
  175.1 1.4 fusion.115
  182.8 1.4 fusion.115
  190.5 1.4 fusion.115
  198.3 1.4 fusion.115
  206.0 1.4 fusion.115
  209.4 26.1 %psum.7 = f32[8,512]{1,0:T(8,128)S(1)} all-reduce(f32[8,512]{1,0:T(8,128)S(1)} %get-tuple-element.262), channel_id=1, replica_groups=mesh['groups'=2,'rows'=4,'mp'=2,'pair'=2] {'rows','pair'}, use_global_device_ids=true, to_apply=%region_15.16 | all-reduce | flops 4096 | bytes 32768 | tf_op jit(solution)/shard_map/psum | solution.py:153
  235.6 97.7 %while.62 = (s32[]{:T(128)}, f32[8,128,256]{2,1,0:T(8,128)S(1)}, bf16[8,512,256]{2,1,0:T(8,128)(2,1)}, bf16[8,512,256]{2,1,0:T(8,128)(2,1)}, s32[8]{0:T(128)S(1)...) while((s32[]{:T(128)}, f32[8,128,256]{2,1,0:T(8,128)S(1)}, ...), condition=%wide.region_19.20_spmd.clone.clone, body=%wide.region_16.19_spmd.clone.sunk.clone | while | flops 673908224 | bytes 7627025 | solution.py:171
  240.1 1.5 fusion.127
  245.8 2.0 fusion.131
  252.3 1.5 fusion.127
  258.0 2.0 fusion.131
  264.5 1.5 fusion.127
  270.2 2.0 fusion.131
  276.7 1.5 fusion.127
  282.4 2.0 fusion.131
  288.9 1.5 fusion.127
  294.7 2.0 fusion.131
  301.1 1.5 fusion.127
  306.9 2.0 fusion.131
  313.3 1.5 fusion.127
  319.1 2.0 fusion.131
  325.5 1.5 fusion.127
  331.3 2.0 fusion.131
  334.3 30.6 %reduce-scatter.2.cloned.1.call-done = f32[128,256]{1,0:T(8,128)} async-done(((f32[1024,256]{1,0:T(8,128)}), f32[128,256]{1,0:T(8,128)}) %reduce-scatter.2.cloned.1.call-update) | async-done | bytes 131088 | tf_op jit(solution)/shard_map/reduce_scatter | solution.py:174
  364.9 1.5 convert_element_type.21
  (263 shorter events, 126.7 us)
Async XLA Ops:
  7.2 357.7 %reduce-scatter.2.cloned.1.call-start = ((), (), s32[]{:S(2)}) async-start(), calls=%async_computation.1 | async-start | bytes 1179648 | tf_op jit(solution)/shard_map/reduce_scatter | solution.py:174
  7.2 22.3 %collective-permute-start = (bf16[128,256]{1,0:T(8,128)(2,1)}, bf16[128,256]{1,0:T(8,128)(2,1)S(1)}, u32[]{:S(2)}, u32[]{:S(2)}) collective-permute-start(bf16[128,256]{1,0:T(8,128)(2,1)} %param.23), channel_id=1, source_target_pairs={{0,1},{1,4},{4,5},{5,8},{8,9},{9,12},{12,13},{13,0},{2,3},{3,6},{6... | collective-permute-start | bytes 196616 | tf_op jit(solution)/shard_map/ppermute | solution.py:60
  29.5 5.5 %collective-permute-start.1 = (bf16[128,256]{1,0:T(8,128)(2,1)S(1)}, bf16[128,256]{1,0:T(8,128)(2,1)S(1)}, u32[]{:S(2)}, u32[]{:S(2)}) collective-permute-start(bf16[128,256]{1,0:T(8,128)(2,1)S(1)} %collective-permute-done), channel_id=1, source_target_pairs={{0,1},{1,4},{4,5},{5,8},{8,9},{9,12},{12,13},{13,0},{2,3},{3,6},{6... | collective-permute-start | bytes 196616 | tf_op jit(solution)/shard_map/ppermute | solution.py:60
  35.0 5.5 %collective-permute-start.2 = (bf16[128,256]{1,0:T(8,128)(2,1)S(1)}, bf16[128,256]{1,0:T(8,128)(2,1)S(1)}, u32[]{:S(2)}, u32[]{:S(2)}) collective-permute-start(bf16[128,256]{1,0:T(8,128)(2,1)S(1)} %collective-permute-done.1), channel_id=1, source_target_pairs={{0,1},{1,4},{4,5},{5,8},{8,9},{9,12},{12,13},{13,0},{2,3},{3,6},{6... | collective-permute-start | bytes 196616 | tf_op jit(solution)/shard_map/ppermute | solution.py:60
  40.5 5.5 %collective-permute-start.3 = (bf16[128,256]{1,0:T(8,128)(2,1)S(1)}, bf16[128,256]{1,0:T(8,128)(2,1)S(1)}, u32[]{:S(2)}, u32[]{:S(2)}) collective-permute-start(bf16[128,256]{1,0:T(8,128)(2,1)S(1)} %collective-permute-done.2), channel_id=1, source_target_pairs={{0,1},{1,4},{4,5},{5,8},{8,9},{9,12},{12,13},{13,0},{2,3},{3,6},{6... | collective-permute-start | bytes 196616 | tf_op jit(solution)/shard_map/ppermute | solution.py:60
  46.0 5.5 %collective-permute-start.4 = (bf16[128,256]{1,0:T(8,128)(2,1)S(1)}, bf16[128,256]{1,0:T(8,128)(2,1)S(1)}, u32[]{:S(2)}, u32[]{:S(2)}) collective-permute-start(bf16[128,256]{1,0:T(8,128)(2,1)S(1)} %collective-permute-done.3), channel_id=1, source_target_pairs={{0,1},{1,4},{4,5},{5,8},{8,9},{9,12},{12,13},{13,0},{2,3},{3,6},{6... | collective-permute-start | bytes 196616 | tf_op jit(solution)/shard_map/ppermute | solution.py:60
  51.5 5.5 %collective-permute-start.5 = (bf16[128,256]{1,0:T(8,128)(2,1)S(1)}, bf16[128,256]{1,0:T(8,128)(2,1)S(1)}, u32[]{:S(2)}, u32[]{:S(2)}) collective-permute-start(bf16[128,256]{1,0:T(8,128)(2,1)S(1)} %collective-permute-done.4), channel_id=1, source_target_pairs={{0,1},{1,4},{4,5},{5,8},{8,9},{9,12},{12,13},{13,0},{2,3},{3,6},{6... | collective-permute-start | bytes 196616 | tf_op jit(solution)/shard_map/ppermute | solution.py:60
  57.0 5.5 %collective-permute-start.6 = (bf16[128,256]{1,0:T(8,128)(2,1)S(1)}, bf16[128,256]{1,0:T(8,128)(2,1)S(1)}, u32[]{:S(2)}, u32[]{:S(2)}) collective-permute-start(bf16[128,256]{1,0:T(8,128)(2,1)S(1)} %collective-permute-done.5), channel_id=1, source_target_pairs={{0,1},{1,4},{4,5},{5,8},{8,9},{9,12},{12,13},{13,0},{2,3},{3,6},{6... | collective-permute-start | bytes 196616 | tf_op jit(solution)/shard_map/ppermute | solution.py:60
  62.5 1.7 copy-start.1
  147.7 87.9 %copy-start.2 = (s32[3]{0:T(128)S(1)}, s32[3]{0:T(128)}, u32[]{:S(2)}) copy-start(s32[3]{0:T(128)} %constant.247.clone.2) | copy-start | bytes 40
  333.3 1.0 copy-start
Sparse Core Ops, SparseCore 0:
  334.4 30.4 reduce-scatter.1
